TPU v7x, 256 devices: a whole 4x4x8 slice. The times are simulated.
256 devices in a mesh: row: 16 (over y, x), col: 8 (over z), chan: 2 (over core).
Axes of the slice: x: 4, y: 4, z: 8, core: 2. Of those that a mesh axis runs over, the one named last changes fastest.
Arguments:
- samples: bfloat16 [8192, 2, 8192], P(('chan', 'col'), None, 'row'), parts along dimension 0, may hold values from -6 to 6
- sky_model: bfloat16 [8192, 2, 4096], P(('chan', 'row'), None, 'col'), parts along dimension 0, may hold values from -128 to 128, as said below
- initial_gains: float32 [2, 8192], P(None, ('chan', 'row', 'col')), parts along dimension 1, may hold values from -3 to 3, as said below
Outputs:
- calibrated: float32 [2, 8192], P(None, ('chan', 'row', 'col')), parts along dimension 1
There are 2 independent parts, one for each index of `chan`. A program takes and returns all parts, laid end to end along the dimension named above; each array names one. Nothing has to cross between parts.
Inputs may be any that keep to these rules, and one draw needn't show every extreme that they name: sky_model is Hermitian: sky_model[q,0,p] = sky_model[p,0,q] and sky_model[q,1,p] = -sky_model[p,1,q]. `initial_gains`: every initial gain has magnitude between 0.3 and 3.
All inputs are finite; a program needn't handle non-finite values.
Results may differ from a plain program's by a relative error of at most 0.0003.
Values may be sent and summed in bfloat16 or wider, within the bound.
No kernel may reach another device: no remote copies, remote signals or barrier semaphores. Data moves between devices by JAX's collectives and lax.ppermute only.
A program may use at most 192 MiB of HBM per device.

v0:
```python
import jax
import jax.numpy as jnp
from jax import lax
from jax.sharding import PartitionSpec as P


def vis_tiles(samples):
    block_column = samples.shape[0]
    flattened = samples.reshape(block_column, -1)
    rotated = jnp.concatenate([-samples[:, 1, :], samples[:, 0, :]], axis=1)
    right_side = jnp.concatenate([flattened, rotated], axis=0)
    all_antennas = lax.all_gather(flattened, "col", axis=0, tiled=True)
    vis_tile = lax.psum_scatter(
        lax.dot_general(
            all_antennas, right_side, (((1,), (1,)), ((), ())), preferred_element_type=jnp.float32
        ),
        "row",
        scatter_dimension=0,
        tiled=True,
    )
    return (vis_tile[:, :block_column], vis_tile[:, block_column:])


def exchange(parts, axis):
    count = lax.axis_size(axis)
    copies = jnp.broadcast_to(parts[None], (count,) + parts.shape)
    return lax.all_to_all(copies, axis, 0, 0)


def columns_to_rows(weight_real, weight_imag, power, gain):
    real = gain[0][None, :]
    imag = gain[1][None, :]
    return jnp.stack(
        [
            jnp.sum(weight_real * real + weight_imag * imag, axis=1),
            jnp.sum(weight_real * imag - weight_imag * real, axis=1),
            jnp.sum(power * (real * real + imag * imag), axis=1),
        ]
    )


def rows_to_columns(weight_real, weight_imag, power, gain):
    real = gain[0][:, None]
    imag = gain[1][:, None]
    return jnp.stack(
        [
            jnp.sum(weight_real * real - weight_imag * imag, axis=0),
            jnp.sum(weight_real * imag + weight_imag * real, axis=0),
            jnp.sum(power * (real * real + imag * imag), axis=0),
        ]
    )


def body(samples, sky_model, initial_gains):
    row_count = lax.axis_size("row")
    column_count = lax.axis_size("col")
    row_index = lax.axis_index("row")
    column_index = lax.axis_index("col")
    block_column = samples.shape[0]
    block_row = sky_model.shape[0]
    share_size = initial_gains.shape[1]
    blocks = block_column // block_row
    everything = lax.all_gather(initial_gains, ("row", "col"), axis=1, tiled=True)
    gain = lax.dynamic_slice_in_dim(everything, column_index * block_column, block_column, 1)
    vis_real, vis_imag = vis_tiles(samples)
    model_real = sky_model[:, 0, :].astype(jnp.float32)
    model_imag = sky_model[:, 1, :].astype(jnp.float32)
    global_rows = row_index * block_row + lax.broadcasted_iota(
        jnp.int32, (block_row, block_column), 0
    )
    global_columns = column_index * block_column + lax.broadcasted_iota(
        jnp.int32, (block_row, block_column), 1
    )
    cross_mask = (global_rows != global_columns).astype(jnp.float32)
    weight_real = (vis_real * model_real + vis_imag * model_imag) * cross_mask
    weight_imag = (vis_real * model_imag - vis_imag * model_real) * cross_mask
    power = (model_real * model_real + model_imag * model_imag) * cross_mask
    parts = columns_to_rows(weight_real, weight_imag, power, gain)
    sums = jnp.sum(exchange(parts, "col"), axis=0)
    gain = sums[:2] / sums[2:]
    parts = rows_to_columns(weight_real, weight_imag, power, gain)
    message = jnp.concatenate([parts.reshape(-1), gain.reshape(-1)])
    message = message.reshape(-1, 128)
    received = exchange(message, "row").reshape(row_count, -1)
    sums = jnp.sum(received[:, : 3 * block_column], axis=0).reshape(3, block_column)
    previous = lax.dynamic_slice_in_dim(
        received[:, 3 * block_column :], column_index * blocks, blocks, 0
    )
    previous = previous.reshape(blocks, 2, block_row).transpose(1, 0, 2).reshape(2, block_column)
    gain = 0.5 * (sums[:2] / sums[2:] + previous)
    parts = columns_to_rows(weight_real, weight_imag, power, gain)
    shares = parts.reshape(3, column_count, share_size).transpose(1, 0, 2)
    sums = jnp.sum(lax.all_to_all(shares, "col", 0, 0), axis=0)
    return sums[:2] / sums[2:]


def solution(mesh):
    return jax.shard_map(
        body,
        mesh=mesh,
        in_specs=(
            P(("chan", "col"), None, "row"),
            P(("chan", "row"), None, "col"),
            P(None, ("chan", "row", "col")),
        ),
        out_specs=P(None, ("chan", "row", "col")),
        check_vma=False,
    )
```

profile of v0, /device:TPU:2, one launch (start us, length us, event | category | flops | bytes accessed | tf_op | source)
XLA Modules:
  0.0 509.9 jit_solution(4030947531042781336)
XLA Ops:
  6.5 0.0 copy-start
  6.5 0.0 all-gather.3.cloned.1.call-start
  6.5 2.6 copy.35
  9.1 0.0 copy-start.1
  9.1 0.0 all-gather.3.cloned.1.call-update
  9.1 0.0 reduce-scatter.2.cloned.1.call-start
  9.2 0.0 copy-done
  9.2 1.5 fusion.11
  10.7 0.1 copy_bitcast_fusion
  10.8 95.5 %all-gather.3.cloned.1.call-done = bf16[4096,1024]{1,0:T(8,128)(2,1)} async-done(((bf16[512,1024]{1,0:T(8,128)(2,1)}), bf16[4096,1024]{1,0:T(8,128)(2,1)}) %all-gather.3.cloned.1.call-update) | async-done | bytes 8388624 | tf_op jit(solution)/shard_map/all_gather | solution.py:12
  106.3 0.0 copy-done.1
  106.3 14.5 %convolution_bitcast_fusion = f32[4096,1024]{0,1:T(8,128)} fusion(bf16[4096,1024]{1,0:T(8,128)(2,1)} %all-gather.3.cloned.1.call-done, bf16[512,512]{1,0:T(8,128)(2,1)S(1)} %get-tuple-element.26, bf16[512,512]{1,0:T(8,128)(2,1)S(1)} %get-tuple-element.27, bf16[512,1024]{1,0:T(8,128)(2,1)S(1)} %bitcast.75), kind=kOutput, calls=%fused_computation | convolution fusion | flops 8596226048 | bytes 27262976 | tf_op jit(solution)/shard_map/dot_general | solution.py:14
  120.8 0.0 copy-start.3
  120.8 0.0 copy-start.2
  120.8 0.0 reduce-scatter.2.cloned.1.call-update
  120.8 0.6 copy-done.3
  121.5 323.6 %all-gather = f32[128,32,2]{1,2,0:T(2,128)S(1)} all-gather(f32[1,32,2]{1,2,0:T(2,128)S(1)} %bitcast.99), channel_id=1, replica_groups=mesh['row'=16,'col'=8,'chan'=2] {'row','col'}, dimensions={0}, use_global_device_ids=true | all-gather | bytes 33024 | tf_op jit(solution)/shard_map/all_gather | solution.py:63
  445.0 0.1 reshape.71
  445.1 0.0 copy-done.2
  445.2 0.7 fusion.12
  445.9 0.5 copy.31
  446.4 0.5 copy.32
  446.9 0.0 reduce-scatter.2.cloned.1.call-done
  446.9 1.7 add_reduce_fusion.2
  448.6 10.4 %all_to_all.15 = f32[8,3,256]{2,1,0:T(4,128)S(1)} all-to-all(f32[8,3,256]{2,1,0:T(4,128)S(1)} %broadcast_in_dim.6), channel_id=1, replica_groups=mesh['row'=16,'col'=8,'chan'=2] {'col'}, dimensions={0} | all-to-all | bytes 49152 | tf_op jit(solution)/shard_map/all_to_all | solution.py:27
  459.1 0.2 multiply_reduce_fusion.1
  459.4 0.3 subtract_reduce_fusion.1
  459.7 0.6 broadcast_in_dim.15
  460.3 24.4 %all-to-all-start.1 = ((f32[16,16,128]{2,1,0:T(8,128)}), f32[16,16,128]{2,1,0:T(8,128)S(1)}, u32[]{:S(2)}, u32[]{:S(2)}) async-start(f32[16,16,128]{2,1,0:T(8,128)} %broadcast_in_dim.15), calls=%async_computation.2 | async-start | bytes 262144 | tf_op jit(solution)/shard_map/all_to_all | solution.py:27
  484.7 6.7 %all-to-all-done.1 = f32[16,16,128]{2,1,0:T(8,128)S(1)} async-done(((f32[16,16,128]{2,1,0:T(8,128)}), f32[16,16,128]{2,1,0:T(8,128)S(1)}, u32[]{:S(2)}, u32[]{:S(2)}) %all-to-all-start.1) | async-done | bytes 131104 | tf_op jit(solution)/shard_map/all_to_all | solution.py:27
  491.6 0.2 add_reduce_fusion
  491.8 0.1 stack.44
  491.9 0.1 stack.45
  492.0 0.2 multiply_reduce_fusion
  492.2 0.1 stack.46
  492.3 10.1 %all_to_all.16 = f32[8,3,32]{2,1,0:T(4,128)S(1)} all-to-all(f32[8,3,32]{2,1,0:T(4,128)S(1)} %maximum_bitcast_fusion), channel_id=1, replica_groups=mesh['row'=16,'col'=8,'chan'=2] {'col'}, dimensions={0} | all-to-all | bytes 6144 | tf_op jit(solution)/shard_map/all_to_all | solution.py:93
  502.5 0.6 slice_divide_fusion.1
  (30 shorter events, 0.3 us)
Async XLA Ops:
  6.5 2.6 copy-start
  6.5 99.8 %all-gather.3.cloned.1.call-start = ((), (), s32[]{:S(2)}) async-start(), calls=%async_computation.4 | async-start | bytes 9437184 | tf_op jit(solution)/shard_map/all_gather | solution.py:12
  9.1 97.2 %copy-start.1 = (bf16[64,8,2,512]{3,1,2,0:T(8,128)(2,1)S(1)}, bf16[64,8,2,512]{3,1,2,0:T(8,128)(2,1)}, u32[]{:S(2)}) copy-start(bf16[64,8,2,512]{3,1,2,0:T(8,128)(2,1)} %copy.35) | copy-start | bytes 3145732
  9.1 437.8 %reduce-scatter.2.cloned.1.call-start = ((), (), s32[]{:S(2)}) async-start(), calls=%async_computation.5 | async-start | bytes 17825792 | tf_op jit(solution)/shard_map/reduce_scatter | solution.py:13
  120.8 0.7 copy-start.3
  120.8 324.4 %copy-start.2 = (bf16[256,2,512]{2,1,0:T(2,128)(2,1)S(1)}, bf16[256,2,512]{2,1,0:T(2,128)(2,1)}, u32[]{:S(2)}) copy-start(bf16[256,2,512]{2,1,0:T(2,128)(2,1)} %param.4) | copy-start | bytes 1572868
  460.3 31.1 %all-to-all-start.1 = ((f32[16,16,128]{2,1,0:T(8,128)}), f32[16,16,128]{2,1,0:T(8,128)S(1)}, u32[]{:S(2)}, u32[]{:S(2)}) async-start(f32[16,16,128]{2,1,0:T(8,128)} %broadcast_in_dim.15), calls=%async_computation.2 | async-start | bytes 262144 | tf_op jit(solution)/shard_map/all_to_all | solution.py:27
Sparse Core Ops, SparseCore 0:
  9.2 97.0 all-gather.2
  120.9 114.0 reduce-scatter.1
where the time goes:
time: 510 us
  blocking collectives  344 us (67%)
  waiting for transfers between devices  102 us (20%)
  starting transfers between devices  24.4 us (5%)
  matrix products  14.5 us (3%)
  between operations  13.7 us (3%)
  local copies, waits for them, and re-layouts  7.56 us (1%)
    all_gather x1, blocking collectives, body(): lax.all_gather(initial_gains, ('row', 'col'), axis=1, tiled=True)  324 us
    all_gather x1, waiting for transfers between devices, vis_tiles(): all_antennas = lax.all_gather(flattened, 'col', axis=0, tiled=True)  95.5 us
    all_to_all x1, starting transfers between devices, exchange(): return lax.all_to_all(copies, axis, 0, 0)  24.4 us
    dot_general x1, matrix products, vis_tiles(): lax.dot_general(all_antennas, right_side, (((1,), (1,)), ((), ())), prefe...  14.5 us
    all_to_all x1, blocking collectives, exchange(): return lax.all_to_all(copies, axis, 0, 0)  10.4 us
  transfers between devices with their start and end apart: 3, of which 2 were waited for; matrix products, arithmetic and copies ran while one was open for 1% of the time, Pallas kernels for 0%

commit v1 on v0

--- a/solution.py
+++ b/solution.py
@@ -1,7 +1,23 @@
+import functools
 import jax
 import jax.numpy as jnp
 from jax import lax
 from jax.sharding import PartitionSpec as P
+
+
+def track_view_up(mine_x, which_axis):
+    return jnp.concatenate(
+        lax.all_to_all(
+            jnp.stack([mine_x] * lax.axis_size(which_axis)),
+            axis_name=which_axis,
+            split_axis=0,
+            concat_axis=0,
+        ),
+        0,
+    )
+
+
+shelves_follow = functools.partial(track_view_up, which_axis="col")
 
 
 def vis_tiles(samples):
@@ -9,7 +25,7 @@
     flattened = samples.reshape(block_column, -1)
     rotated = jnp.concatenate([-samples[:, 1, :], samples[:, 0, :]], axis=1)
     right_side = jnp.concatenate([flattened, rotated], axis=0)
-    all_antennas = lax.all_gather(flattened, "col", axis=0, tiled=True)
+    all_antennas = shelves_follow(flattened)
     vis_tile = lax.psum_scatter(
         lax.dot_general(
             all_antennas, right_side, (((1,), (1,)), ((), ())), preferred_element_type=jnp.float32

time: 510 us -> 607 us (1.19)
  waiting for transfers between devices: 102 us -> 192 us
  starting transfers between devices: 24.4 us -> 33 us
    all_to_all x0 -> x1, waiting for transfers between devices: none -> 185 us  [track_view_up(): lax.all_to_all(jnp.stack([mine_x] * lax.axis_size(which_axis)), axis_name...]
    all_gather x1 -> x0, waiting for transfers between devices: 95.5 us -> none  [vis_tiles(): all_antennas = lax.all_gather(flattened, 'col', axis=0, tiled=True)]
    all_to_all x0 -> x1, starting transfers between devices: none -> 8.6 us  [track_view_up(): lax.all_to_all(jnp.stack([mine_x] * lax.axis_size(which_axis)), axis_name...]
where the time goes in v1:
time: 607 us; the launch traced here: 606 us
  blocking collectives  339 us (56%)
  waiting for transfers between devices  192 us (32%)
  starting transfers between devices  33 us (5%)
  matrix products  14.5 us (2%)
  between operations  13.7 us (2%)
  local copies, waits for them, and re-layouts  10.8 us (2%)
    all_gather x1, blocking collectives, body(): lax.all_gather(initial_gains, ('row', 'col'), axis=1, tiled=True)  318 us
    all_to_all x1, waiting for transfers between devices, track_view_up(): lax.all_to_all(jnp.stack([mine_x] * lax.axis_size(which_axis)), axis_name...  185 us
    all_to_all x1, starting transfers between devices, exchange(): return lax.all_to_all(copies, axis, 0, 0)  24.4 us
    dot_general x1, matrix products, vis_tiles(): lax.dot_general(all_antennas, right_side, (((1,), (1,)), ((), ())), prefe...  14.5 us
  transfers between devices with their start and end apart: 3, of which 2 were waited for; matrix products, arithmetic and copies ran while one was open for 1% of the time, Pallas kernels for 0%

profile of v1, /device:TPU:2, one launch (start us, length us, event | category | flops | bytes accessed | tf_op | source)
XLA Modules:
  0.0 606.2 jit_solution(4252811817936998913)
XLA Ops:
  6.5 1.5 copy.35
  8.0 4.3 stack.39
  12.3 0.0 copy-start
  12.3 8.6 %all-to-all-start = ((bf16[8,512,1024]{2,1,0:T(8,128)(2,1)}), bf16[8,512,1024]{2,1,0:T(8,128)(2,1)}, u32[]{:S(2)}, u32[]{:S(2)}) async-start(bf16[8,512,1024]{2,1,0:T(8,128)(2,1)} %stack.39), calls=%async_computation | async-start | bytes 16777216 | tf_op jit(solution)/shard_map/all_to_all | solution.py:10
  20.9 0.0 reduce-scatter.2.cloned.1.call-start
  21.0 0.0 copy-done
  21.0 1.5 fusion.11
  22.5 0.1 copy_bitcast_fusion
  22.6 184.9 %all-to-all-done = bf16[8,512,1024]{2,1,0:T(8,128)(2,1)} async-done(((bf16[8,512,1024]{2,1,0:T(8,128)(2,1)}), bf16[8,512,1024]{2,1,0:T(8,128)(2,1)}, u32[]{:S(2)}, u32[]{:S(2)}) %all-to-all-start) | async-done | bytes 8388640 | tf_op jit(solution)/shard_map/all_to_all | solution.py:10
  207.5 14.5 %convolution_bitcast_fusion = f32[4096,1024]{0,1:T(8,128)} fusion(bf16[4096,1024]{1,0:T(8,128)(2,1)} %bitcast.2, bf16[512,512]{1,0:T(8,128)(2,1)S(1)} %get-tuple-element.26, bf16[512,512]{1,0:T(8,128)(2,1)S(1)} %get-tuple-element.27, bf16[512,1024]{1,0:T(8,128)(2,1)S(1)} %bitcast.76), kind=kOutput, calls=%fused_computation | convolution fusion | flops 8596226048 | bytes 27262976 | tf_op jit(solution)/shard_map/dot_general | solution.py:30
  222.0 0.0 copy-start.2
  222.0 0.0 copy-start.1
  222.0 0.0 reduce-scatter.2.cloned.1.call-update
  222.0 0.6 copy-done.2
  222.7 318.0 %all-gather = f32[128,32,2]{1,2,0:T(2,128)S(1)} all-gather(f32[1,32,2]{1,2,0:T(2,128)S(1)} %bitcast.100), channel_id=1, replica_groups=mesh['row'=16,'col'=8,'chan'=2] {'row','col'}, dimensions={0}, use_global_device_ids=true | all-gather | bytes 33024 | tf_op jit(solution)/shard_map/all_gather | solution.py:79
  540.7 0.1 reshape.77
  540.8 0.0 copy-done.1
  540.8 0.7 fusion.12
  541.5 0.5 copy.31
  542.0 0.5 copy.32
  542.6 0.0 reduce-scatter.2.cloned.1.call-done
  542.6 1.7 add_reduce_fusion.2
  544.3 11.0 %all_to_all.20 = f32[8,3,256]{2,1,0:T(4,128)S(1)} all-to-all(f32[8,3,256]{2,1,0:T(4,128)S(1)} %broadcast_in_dim.6), channel_id=1, replica_groups=mesh['row'=16,'col'=8,'chan'=2] {'col'}, dimensions={0} | all-to-all | bytes 49152 | tf_op jit(solution)/shard_map/all_to_all | solution.py:43
  555.4 0.2 multiply_reduce_fusion.1
  555.7 0.2 subtract_reduce_fusion.1
  556.0 0.6 broadcast_in_dim.15
  556.6 24.4 %all-to-all-start.2 = ((f32[16,16,128]{2,1,0:T(8,128)}), f32[16,16,128]{2,1,0:T(8,128)S(1)}, u32[]{:S(2)}, u32[]{:S(2)}) async-start(f32[16,16,128]{2,1,0:T(8,128)} %broadcast_in_dim.15), calls=%async_computation.3 | async-start | bytes 262144 | tf_op jit(solution)/shard_map/all_to_all | solution.py:43
  581.0 6.7 %all-to-all-done.2 = f32[16,16,128]{2,1,0:T(8,128)S(1)} async-done(((f32[16,16,128]{2,1,0:T(8,128)}), f32[16,16,128]{2,1,0:T(8,128)S(1)}, u32[]{:S(2)}, u32[]{:S(2)}) %all-to-all-start.2) | async-done | bytes 131104 | tf_op jit(solution)/shard_map/all_to_all | solution.py:43
  587.9 0.2 add_reduce_fusion
  588.1 0.1 stack.48
  588.2 0.1 stack.49
  588.3 0.2 multiply_reduce_fusion
  588.5 0.1 stack.50
  588.6 10.1 %all_to_all.21 = f32[8,3,32]{2,1,0:T(4,128)S(1)} all-to-all(f32[8,3,32]{2,1,0:T(4,128)S(1)} %maximum_bitcast_fusion), channel_id=1, replica_groups=mesh['row'=16,'col'=8,'chan'=2] {'col'}, dimensions={0} | all-to-all | bytes 6144 | tf_op jit(solution)/shard_map/all_to_all | solution.py:109
  598.8 0.6 slice_divide_fusion.1
  (30 shorter events, 0.3 us)
Async XLA Ops:
  12.3 8.6 %copy-start = (bf16[512,2,512]{2,1,0:T(2,128)(2,1)S(1)}, bf16[512,2,512]{2,1,0:T(2,128)(2,1)}, u32[]{:S(2)}) copy-start(bf16[512,2,512]{2,1,0:T(2,128)(2,1)} %param.3) | copy-start | bytes 3145732
  12.3 195.2 %all-to-all-start = ((bf16[8,512,1024]{2,1,0:T(8,128)(2,1)}), bf16[8,512,1024]{2,1,0:T(8,128)(2,1)}, u32[]{:S(2)}, u32[]{:S(2)}) async-start(bf16[8,512,1024]{2,1,0:T(8,128)(2,1)} %stack.39), calls=%async_computation | async-start | bytes 16777216 | tf_op jit(solution)/shard_map/all_to_all | solution.py:10
  20.9 521.7 %reduce-scatter.2.cloned.1.call-start = ((), (), s32[]{:S(2)}) async-start(), calls=%async_computation.5 | async-start | bytes 17825792 | tf_op jit(solution)/shard_map/reduce_scatter | solution.py:29
  222.0 0.7 copy-start.2
  222.0 318.8 %copy-start.1 = (bf16[256,2,512]{2,1,0:T(2,128)(2,1)S(1)}, bf16[256,2,512]{2,1,0:T(2,128)(2,1)}, u32[]{:S(2)}) copy-start(bf16[256,2,512]{2,1,0:T(2,128)(2,1)} %param.4) | copy-start | bytes 1572868
  556.6 31.1 %all-to-all-start.2 = ((f32[16,16,128]{2,1,0:T(8,128)}), f32[16,16,128]{2,1,0:T(8,128)S(1)}, u32[]{:S(2)}, u32[]{:S(2)}) async-start(f32[16,16,128]{2,1,0:T(8,128)} %broadcast_in_dim.15), calls=%async_computation.3 | async-start | bytes 262144 | tf_op jit(solution)/shard_map/all_to_all | solution.py:43
Sparse Core Ops, SparseCore 0:
  222.2 111.7 reduce-scatter.1
